TPU v7x, 256 devices: a whole 4x4x8 slice. The times are simulated.
256 devices in a mesh: ctx: 64 (over z, x, core), heads: 4 (over y).
Axes of the slice: x: 4, y: 4, z: 8, core: 2. Of those that a mesh axis runs over, the one named last changes fastest.
Arguments:
- q_raw: bfloat16 [16384, 8192], P('ctx', 'heads'), may hold values from -60 to 60
- k_raw: bfloat16 [16384, 1024], P('ctx', 'heads'), may hold values from -60 to 60
- values: bfloat16 [16384, 1024], P('ctx', 'heads'), may hold values from -6 to 6
- saved_out: bfloat16 [16384, 8192], P('ctx', 'heads'), may hold values from -6 to 6
- out_grad: bfloat16 [16384, 8192], P('ctx', 'heads'), may hold values from -60 to 60
- q_gain: float32 [128], replicated, may hold values from 0.25 to 1.75
- k_gain: float32 [128], replicated, may hold values from 0.25 to 1.75
- ancestors: int32 [256, 32], P('ctx'), may hold values from -1 to 255, as said below
Outputs:
- dq_raw: bfloat16 [16384, 8192], P('ctx', 'heads')
- dk_raw: bfloat16 [16384, 1024], P('ctx', 'heads')
- dv: bfloat16 [16384, 1024], P('ctx', 'heads')
- q_gain_grad: float32 [128], replicated
- k_gain_grad: float32 [128], replicated
Inputs may be any that keep to these rules, and one draw needn't show every extreme that they name: `ancestors`: the forest is 8 trees of 32 blocks each; in tree order, tree k holds blocks (k * 32 + 256 / 64 + b) mod 256 for b = 0 to 31. Row b lists, in tree order, every block on the path from its tree's first block to b, ending with b itself, then -1s. The first 16 blocks of a tree form its prompt, each the child of the block before it; every other block's parent is a block earlier in its tree, from the prompt's last block on.
All inputs are finite; a program needn't handle non-finite values.
Results may differ from a plain program's by a relative error of at most 0.0069.
Values may be sent and summed in bfloat16 or wider, within the bound.
A program may use at most 64 MiB of HBM per device.

v0:
```python
import math
import jax
import jax.numpy as jnp
from jax import lax
from jax.sharding import PartitionSpec as P

TREE_DEV = 8
ROPE_BASE = 1000000.0
EPS = 1e-06


def passed_along(value, axis, steps):
    count = lax.axis_size(axis)
    pairs = [(source, (source + steps) % count) for source in range(count)]
    return lax.ppermute(value, axis, pairs)


def rope_tables(positions, head_dim):
    half_dim = head_dim // 2
    frequency = jnp.exp(
        jnp.arange(half_dim, dtype=jnp.float32) * (-2.0 * math.log(ROPE_BASE) / head_dim)
    )
    angles = positions.astype(jnp.float32)[:, None] * frequency[None, :]
    return (jnp.cos(angles), jnp.sin(angles))


def norm_rope(inputs, gain_vec, cos_table, sin_table):
    recip_rms = lax.rsqrt(jnp.mean(inputs * inputs, -1, keepdims=True) + EPS)
    scaled = inputs * recip_rms * gain_vec
    half_dim = inputs.shape[-1] // 2
    cos_part = cos_table[:, None, :]
    sin_part = sin_table[:, None, :]
    front_half = scaled[..., :half_dim]
    back_half = scaled[..., half_dim:]
    return jnp.concatenate(
        [
            front_half * cos_part - back_half * sin_part,
            back_half * cos_part + front_half * sin_part,
        ],
        -1,
    )


def norm_rope_back(inputs, gain_vec, cos_table, sin_table, upstream):
    half_dim = inputs.shape[-1] // 2
    cos_part = cos_table[:, None, :]
    sin_part = sin_table[:, None, :]
    front_half = upstream[..., :half_dim]
    back_half = upstream[..., half_dim:]
    unrotated = jnp.concatenate(
        [
            front_half * cos_part + back_half * sin_part,
            back_half * cos_part - front_half * sin_part,
        ],
        -1,
    )
    recip_rms = lax.rsqrt(jnp.mean(inputs * inputs, -1, keepdims=True) + EPS)
    normed = inputs * recip_rms
    gain_term = jnp.sum(unrotated * normed, axis=(0, 1))
    gain_grad = unrotated * gain_vec
    input_grad = recip_rms * (gain_grad - normed * jnp.mean(gain_grad * normed, -1, keepdims=True))
    return (input_grad, gain_term)


def on_device(q_raw, k_raw, values, saved_out, out_grad, q_gain, k_gain, ancestors):
    tokens_here = q_raw.shape[0]
    head_dim = q_gain.shape[0]
    kv_local = k_raw.shape[1] // head_dim
    group_size = q_raw.shape[1] // (kv_local * head_dim)
    block_count = ancestors.shape[0]
    block_len = tokens_here // block_count
    cycle_size = lax.axis_size("ctx")
    my_index = lax.axis_index("ctx")
    hop_count = TREE_DEV - 1
    inv_root = 1.0 / math.sqrt(head_dim)
    offsets = jnp.arange(block_len, dtype=jnp.int32)
    depth_count = jnp.sum((ancestors >= 0).astype(jnp.int32), 1)
    positions = (((depth_count - 1) * block_len)[:, None] + offsets[None, :]).reshape(tokens_here)
    cos_table, sin_table = rope_tables(positions, head_dim)
    q_float = q_raw.astype(jnp.float32).reshape(tokens_here, kv_local * group_size, head_dim)
    k_float = k_raw.astype(jnp.float32).reshape(tokens_here, kv_local, head_dim)
    q_rot = norm_rope(q_float, q_gain, cos_table, sin_table).astype(jnp.bfloat16)
    q_rot = q_rot.reshape(tokens_here, kv_local, group_size, head_dim)
    k_rot = norm_rope(k_float, k_gain, cos_table, sin_table).astype(jnp.bfloat16)
    v_heads = values.reshape(tokens_here, kv_local, head_dim)
    grad_heads = out_grad.reshape(tokens_here, kv_local, group_size, head_dim)
    out_heads = saved_out.reshape(tokens_here, kv_local, group_size, head_dim)
    row_delta = jnp.einsum(
        "ikgd,ikgd->kgi", grad_heads, out_heads, preferred_element_type=jnp.float32
    )
    key_value = jnp.stack((k_rot, v_heads), 1)
    local_tok = jnp.arange(tokens_here, dtype=jnp.int32)

    def visible(source):
        key_blocks = source * block_count + jnp.arange(block_count, dtype=jnp.int32)
        block_vis = jnp.any(ancestors[:, :, None] == key_blocks[None, None, :], axis=1)
        token_vis = jnp.repeat(jnp.repeat(block_vis, block_len, 0), block_len, 1)
        causal = (local_tok[None, :] <= local_tok[:, None]) | (source != my_index)
        return (token_vis & causal, jnp.any(block_vis))

    def scores_of(key_rot):
        return (
            jnp.einsum("ikgd,jkd->kgij", q_rot, key_rot, preferred_element_type=jnp.float32)
            * inv_root
        )

    def add_mass(exp_mass, key_rot, allowed):
        expo = jnp.where(allowed[None, None], jnp.exp(scores_of(key_rot)), 0.0)
        return exp_mass + jnp.sum(expo, -1)

    def accumulate(exp_mass, key_rot, allowed):
        return add_mass(exp_mass, key_rot, allowed)

    own_allowed, own_touched = visible(my_index)
    exp_mass = add_mass(
        jnp.zeros((kv_local, group_size, tokens_here), jnp.float32), k_rot, own_allowed
    )

    def forward_step(hop_index, loop_state):
        mass_now, moving = loop_state
        moving = passed_along(moving, "ctx", 1)
        allowed, touched = visible((my_index - hop_index) % cycle_size)
        return (accumulate(mass_now, moving, allowed), moving)

    exp_mass, _ = lax.fori_loop(1, hop_count + 1, forward_step, (exp_mass, k_rot))
    log_mass = jnp.log(exp_mass)

    def grad_terms(key_rot, val_rot, allowed):
        weights = jnp.where(
            allowed[None, None], jnp.exp(scores_of(key_rot) - log_mass[..., None]), 0.0
        )
        weights_low = weights.astype(jnp.bfloat16)
        grad_prob = jnp.einsum(
            "ikgd,jkd->kgij", grad_heads, val_rot, preferred_element_type=jnp.float32
        )
        dscore = (weights * (grad_prob - row_delta[..., None]) * inv_root).astype(jnp.bfloat16)
        dq_part = jnp.einsum("kgij,jkd->ikgd", dscore, key_rot, preferred_element_type=jnp.float32)
        dk_part = jnp.einsum("kgij,ikgd->jkd", dscore, q_rot, preferred_element_type=jnp.float32)
        dv_part = jnp.einsum(
            "kgij,ikgd->jkd", weights_low, grad_heads, preferred_element_type=jnp.float32
        )
        return (dq_part, jnp.stack((dk_part, dv_part), 1))

    def pair_terms(moving, allowed):
        return grad_terms(moving[:, 0], moving[:, 1], allowed)

    dq_acc, own_part = grad_terms(k_rot, v_heads, own_allowed)
    key_grads = own_part

    def back_step(hop_index, loop_state):
        dq_now, grads_now, moving = loop_state
        moving = passed_along(moving, "ctx", 1)
        source = (my_index - hop_index) % cycle_size
        allowed, touched = visible(source)
        dq_part, kv_part = pair_terms(moving, allowed)
        grads_now = passed_along(grads_now, "ctx", 1) + kv_part
        return (dq_now + dq_part, grads_now, moving)

    dq_acc, key_grads, _ = lax.fori_loop(
        1, hop_count + 1, back_step, (dq_acc, key_grads, key_value)
    )
    key_grads = passed_along(key_grads, "ctx", -hop_count)
    dq_rot = dq_acc.reshape(tokens_here, kv_local * group_size, head_dim)
    dq_input, q_gain_part = norm_rope_back(q_float, q_gain, cos_table, sin_table, dq_rot)
    dk_input, k_gain_part = norm_rope_back(k_float, k_gain, cos_table, sin_table, key_grads[:, 0])
    q_gain_grad, k_gain_grad = lax.psum((q_gain_part, k_gain_part), ("ctx", "heads"))
    dq_raw = dq_input.astype(jnp.bfloat16).reshape(tokens_here, kv_local * group_size * head_dim)
    dk_raw = dk_input.astype(jnp.bfloat16).reshape(tokens_here, kv_local * head_dim)
    dv = key_grads[:, 1].astype(jnp.bfloat16).reshape(tokens_here, kv_local * head_dim)
    return (dq_raw, dk_raw, dv, q_gain_grad, k_gain_grad)


def solution(mesh):
    in_specs = (
        P("ctx", "heads"),
        P("ctx", "heads"),
        P("ctx", "heads"),
        P("ctx", "heads"),
        P("ctx", "heads"),
        P(),
        P(),
        P("ctx", None),
    )
    out_specs = (P("ctx", "heads"), P("ctx", "heads"), P("ctx", "heads"), P(), P())
    return jax.shard_map(
        on_device, mesh=mesh, in_specs=in_specs, out_specs=out_specs, check_vma=False
    )
```

profile of v0, /device:TPU:1, one launch (start us, length us, event | category | flops | bytes accessed | tf_op | source)
XLA Modules:
  0.0 316.6 jit_solution(3900875006757037314)
XLA Ops:
  2.8 1.5 convert_bitcast_fusion
  11.5 2.9 fusion.29
  14.4 59.1 %while.38 = (s32[]{:T(128)}, f32[2,8,256]{2,1,0:T(8,128)S(1)}, bf16[256,2,128]{2,0,1:T(8,128)(2,1)S(1)}, s32[4,32]{1,0:T(4,128)S(1)}, s32[]{:T(128)}, /*index=5*...) while((s32[]{:T(128)}, f32[2,8,256]{2,1,0:T(8,128)S(1)}, ...), condition=%wide.region_8.9_spmd.clone, body=%wide.region_5.8_spmd.clone.sunk | while | flops 271778816 | bytes 2167688 | solution.py:125
  14.4 2.6 collective-permute-start
  20.0 2.5 collective-permute-start
  23.1 4.9 %collective-permute-done = bf16[256,2,128]{2,0,1:T(8,128)(2,1)S(1)} collective-permute-done((bf16[256,2,128]{2,0,1:T(8,128)(2,1)S(1)}, bf16[256,2,128]{2,0,1:T(8,128)(2,1)S(1)}, u32[]{:S(2)}, u32[]{:S(2)}) %collective-permute-start) | collective-permute-done | bytes 131104 | tf_op jit(solution)/shard_map/while/body/eval_jaxpr/ppermute | solution.py:15
  29.8 7.1 %collective-permute-done = bf16[256,2,128]{2,0,1:T(8,128)(2,1)S(1)} collective-permute-done((bf16[256,2,128]{2,0,1:T(8,128)(2,1)S(1)}, bf16[256,2,128]{2,0,1:T(8,128)(2,1)S(1)}, u32[]{:S(2)}, u32[]{:S(2)}) %collective-permute-start) | collective-permute-done | bytes 131104 | tf_op jit(solution)/shard_map/while/body/eval_jaxpr/ppermute | solution.py:15
  38.7 7.1 %collective-permute-done = bf16[256,2,128]{2,0,1:T(8,128)(2,1)S(1)} collective-permute-done((bf16[256,2,128]{2,0,1:T(8,128)(2,1)S(1)}, bf16[256,2,128]{2,0,1:T(8,128)(2,1)S(1)}, u32[]{:S(2)}, u32[]{:S(2)}) %collective-permute-start) | collective-permute-done | bytes 131104 | tf_op jit(solution)/shard_map/while/body/eval_jaxpr/ppermute | solution.py:15
  47.5 7.1 %collective-permute-done = bf16[256,2,128]{2,0,1:T(8,128)(2,1)S(1)} collective-permute-done((bf16[256,2,128]{2,0,1:T(8,128)(2,1)S(1)}, bf16[256,2,128]{2,0,1:T(8,128)(2,1)S(1)}, u32[]{:S(2)}, u32[]{:S(2)}) %collective-permute-start) | collective-permute-done | bytes 131104 | tf_op jit(solution)/shard_map/while/body/eval_jaxpr/ppermute | solution.py:15
  56.4 7.1 %collective-permute-done = bf16[256,2,128]{2,0,1:T(8,128)(2,1)S(1)} collective-permute-done((bf16[256,2,128]{2,0,1:T(8,128)(2,1)S(1)}, bf16[256,2,128]{2,0,1:T(8,128)(2,1)S(1)}, u32[]{:S(2)}, u32[]{:S(2)}) %collective-permute-start) | collective-permute-done | bytes 131104 | tf_op jit(solution)/shard_map/while/body/eval_jaxpr/ppermute | solution.py:15
  65.3 7.1 %collective-permute-done = bf16[256,2,128]{2,0,1:T(8,128)(2,1)S(1)} collective-permute-done((bf16[256,2,128]{2,0,1:T(8,128)(2,1)S(1)}, bf16[256,2,128]{2,0,1:T(8,128)(2,1)S(1)}, u32[]{:S(2)}, u32[]{:S(2)}) %collective-permute-start) | collective-permute-done | bytes 131104 | tf_op jit(solution)/shard_map/while/body/eval_jaxpr/ppermute | solution.py:15
  74.6 1.9 copy.122
  79.2 3.3 %fusion.40 = f32[256,1,2,128]{0,3,2,1:T(8,128)S(1)} fusion(bf16[256,2,8,128]{0,3,2,1:T(8,128)(2,1)S(1)} %bitcast.262, f32[2,256,256,8]{2,1,3,0:T(8,128)} %get-tuple-element.597, f32[2,8,256]{2,1,0:T(8,128)S(1)} %copy-done.24, pred[256,256]{0,1:T(8,128)(4,1)S(1)} %copy-done.21), kind=kOutput, calls=%fused_computation.66 | convolution fusion | flops 272629760 | bytes 5586944 | tf_op jit(solution)/shard_map/kgij,ikgd->jkd/dot_general | solution.py:139
  82.6 1.5 fusion.27
  85.0 1.8 convolution_bitcast_fusion.1
  89.9 1.9 copy.98
  91.8 1.7 copy.97
  93.5 1.7 pad_maximum_fusion.3
  95.2 123.4 %while.39 = (s32[]{:T(128)}, f32[256,2,8,128]{3,0,2,1:T(8,128)S(1)}, f32[256,2,2,128]{3,0,2,1:T(8,128)}, bf16[256,2,2,128]{3,0,2,1:T(8,128)(2,1)}, s32[4,32]{1,0...) while((s32[]{:T(128)}, ...), condition=%wide.region_11.12_spmd.clone, body=%wide.region_9.11_spmd.clone.sunk | while | flops 1354695680 | bytes 37999652 | solution.py:159
  96.9 6.4 %collective-permute-done.1 = bf16[256,2,2,128]{3,0,2,1:T(8,128)(2,1)S(1)} collective-permute-done((bf16[256,2,2,128]{3,0,2,1:T(8,128)(2,1)}, bf16[256,2,2,128]{3,0,2,1:T(8,128)(2,1)S(1)}, u32[]{:S(2)}, u32[]{:S(2)}) %collective-permute-start.1) | collective-permute-done | bytes 262176 | tf_op jit(solution)/shard_map/while/body/eval_jaxpr/ppermute | solution.py:15
  104.6 1.5 fusion.95
  106.1 1.4 bitcast_add_fusion.2
  109.9 1.9 maximum_add_fusion.2
  113.5 7.6 %collective-permute-done.1 = bf16[256,2,2,128]{3,0,2,1:T(8,128)(2,1)S(1)} collective-permute-done((bf16[256,2,2,128]{3,0,2,1:T(8,128)(2,1)}, bf16[256,2,2,128]{3,0,2,1:T(8,128)(2,1)S(1)}, u32[]{:S(2)}, u32[]{:S(2)}) %collective-permute-start.1) | collective-permute-done | bytes 262176 | tf_op jit(solution)/shard_map/while/body/eval_jaxpr/ppermute | solution.py:15
  122.4 1.5 fusion.95
  123.9 1.4 bitcast_add_fusion.2
  127.7 1.9 maximum_add_fusion.2
  131.3 7.6 %collective-permute-done.1 = bf16[256,2,2,128]{3,0,2,1:T(8,128)(2,1)S(1)} collective-permute-done((bf16[256,2,2,128]{3,0,2,1:T(8,128)(2,1)}, bf16[256,2,2,128]{3,0,2,1:T(8,128)(2,1)S(1)}, u32[]{:S(2)}, u32[]{:S(2)}) %collective-permute-start.1) | collective-permute-done | bytes 262176 | tf_op jit(solution)/shard_map/while/body/eval_jaxpr/ppermute | solution.py:15
  140.2 1.5 fusion.95
  145.5 1.9 maximum_add_fusion.2
  149.1 7.6 %collective-permute-done.1 = bf16[256,2,2,128]{3,0,2,1:T(8,128)(2,1)S(1)} collective-permute-done((bf16[256,2,2,128]{3,0,2,1:T(8,128)(2,1)}, bf16[256,2,2,128]{3,0,2,1:T(8,128)(2,1)S(1)}, u32[]{:S(2)}, u32[]{:S(2)}) %collective-permute-start.1) | collective-permute-done | bytes 262176 | tf_op jit(solution)/shard_map/while/body/eval_jaxpr/ppermute | solution.py:15
  158.0 1.5 fusion.95
  159.5 1.4 bitcast_add_fusion.2
  163.3 1.9 maximum_add_fusion.2
  166.9 7.6 %collective-permute-done.1 = bf16[256,2,2,128]{3,0,2,1:T(8,128)(2,1)S(1)} collective-permute-done((bf16[256,2,2,128]{3,0,2,1:T(8,128)(2,1)}, bf16[256,2,2,128]{3,0,2,1:T(8,128)(2,1)S(1)}, u32[]{:S(2)}, u32[]{:S(2)}) %collective-permute-start.1) | collective-permute-done | bytes 262176 | tf_op jit(solution)/shard_map/while/body/eval_jaxpr/ppermute | solution.py:15
  175.8 1.5 fusion.95
  181.1 1.9 maximum_add_fusion.2
  184.7 7.6 %collective-permute-done.1 = bf16[256,2,2,128]{3,0,2,1:T(8,128)(2,1)S(1)} collective-permute-done((bf16[256,2,2,128]{3,0,2,1:T(8,128)(2,1)}, bf16[256,2,2,128]{3,0,2,1:T(8,128)(2,1)S(1)}, u32[]{:S(2)}, u32[]{:S(2)}) %collective-permute-start.1) | collective-permute-done | bytes 262176 | tf_op jit(solution)/shard_map/while/body/eval_jaxpr/ppermute | solution.py:15
  193.6 1.5 fusion.95
  195.1 1.4 bitcast_add_fusion.2
  198.9 1.9 maximum_add_fusion.2
  202.5 7.6 %collective-permute-done.1 = bf16[256,2,2,128]{3,0,2,1:T(8,128)(2,1)S(1)} collective-permute-done((bf16[256,2,2,128]{3,0,2,1:T(8,128)(2,1)}, bf16[256,2,2,128]{3,0,2,1:T(8,128)(2,1)S(1)}, u32[]{:S(2)}, u32[]{:S(2)}) %collective-permute-start.1) | collective-permute-done | bytes 262176 | tf_op jit(solution)/shard_map/while/body/eval_jaxpr/ppermute | solution.py:15
  211.4 1.5 fusion.95
  216.7 1.9 maximum_add_fusion.2
  220.2 2.5 multiply_add_fusion
  222.7 2.1 multiply_reduce_fusion.1
  226.0 3.8 %fusion.36 = (f32[2048]{0:T(1024)S(1)}, bf16[256,2048]{1,0:T(8,128)(2,1)}) fusion(bf16[256,2048]{1,0:T(8,128)(2,1)S(1)} %copy-done.3, f32[32,8,16,128]{3,2,1,0:T(8,128)S(1)} %bitcast.265, f32[32,8,16,128]{3,2,1,0:T(8,128)S(1)} %bitcast.267, f32[32,8,16,128]{3,2,1,0:T(8,128)S(1)} %bitcast.266, f32[2048]{0:T(1024)S(1)} %broadcast_bitcast_fusion), kind=kLoop, calls=%fused_computation.53 | loop fusion | flops 4716544 | bytes 8404992 | tf_op jit(solution)/shard_map/reduce_sum | solution.py:59
  232.6 84.0 %all-reduce = (f32[128]{0:T(128)}, f32[128]{0:T(128)}) all-reduce(f32[128]{0:T(128)S(1)} %bitcast_reduce_fusion, f32[128]{0:T(128)S(1)} %bitcast_reduce_fusion.1), channel_id=1, replica_groups=mesh['ctx'=64,'heads'=4] {'ctx','heads'}, use_global_device_ids=true, to_apply=%region_16.17 | all-reduce | flops 256 | bytes 2048 | tf_op jit(solution)/shard_map/psum | solution.py:166
  (320 shorter events, 76.7 us)
Async XLA Ops:
  1.7 3.0 copy-start.10
  1.8 5.1 %copy-start.6 = (f32[256,2,128]{2,0,1:T(8,128)}, f32[256,2,128]{2,0,1:T(8,128)S(1)}, u32[]{:S(2)}) copy-start(f32[256,2,128]{2,0,1:T(8,128)S(1)} %copy.83) | copy-start | bytes 786436
  4.7 2.2 copy-start
  4.7 1.3 copy-start.26
  7.3 2.6 copy-start.12
  11.5 2.9 copy-start.19
  14.4 59.7 %copy-start.14 = (bf16[256,2048]{1,0:T(8,128)(2,1)S(1)}, bf16[256,2048]{1,0:T(8,128)(2,1)}, u32[]{:S(2)}) copy-start(bf16[256,2048]{1,0:T(8,128)(2,1)} %param.16) | copy-start | bytes 3145732
  14.4 4.5 %collective-permute-start = (bf16[256,2,128]{2,0,1:T(8,128)(2,1)S(1)}, bf16[256,2,128]{2,0,1:T(8,128)(2,1)S(1)}, u32[]{:S(2)}, u32[]{:S(2)}) collective-permute-start(bf16[256,2,128]{2,0,1:T(8,128)(2,1)S(1)} %get-tuple-element.709), channel_id=1, source_target_pairs={{0,4},{4,8},{8,12},{12,16},{16,20},{20,24},{24,28},{28,32},{32,36}... | collective-permute-start | bytes 393224 | tf_op jit(solution)/shard_map/while/body/eval_jaxpr/ppermute | solution.py:15
  20.0 8.0 %collective-permute-start = (bf16[256,2,128]{2,0,1:T(8,128)(2,1)S(1)}, bf16[256,2,128]{2,0,1:T(8,128)(2,1)S(1)}, u32[]{:S(2)}, u32[]{:S(2)}) collective-permute-start(bf16[256,2,128]{2,0,1:T(8,128)(2,1)S(1)} %get-tuple-element.709), channel_id=1, source_target_pairs={{0,4},{4,8},{8,12},{12,16},{16,20},{20,24},{24,28},{28,32},{32,36}... | collective-permute-start | bytes 393224 | tf_op jit(solution)/shard_map/while/body/eval_jaxpr/ppermute | solution.py:15
  29.1 7.8 %collective-permute-start = (bf16[256,2,128]{2,0,1:T(8,128)(2,1)S(1)}, bf16[256,2,128]{2,0,1:T(8,128)(2,1)S(1)}, u32[]{:S(2)}, u32[]{:S(2)}) collective-permute-start(bf16[256,2,128]{2,0,1:T(8,128)(2,1)S(1)} %get-tuple-element.709), channel_id=1, source_target_pairs={{0,4},{4,8},{8,12},{12,16},{16,20},{20,24},{24,28},{28,32},{32,36}... | collective-permute-start | bytes 393224 | tf_op jit(solution)/shard_map/while/body/eval_jaxpr/ppermute | solution.py:15
  38.0 7.8 %collective-permute-start = (bf16[256,2,128]{2,0,1:T(8,128)(2,1)S(1)}, bf16[256,2,128]{2,0,1:T(8,128)(2,1)S(1)}, u32[]{:S(2)}, u32[]{:S(2)}) collective-permute-start(bf16[256,2,128]{2,0,1:T(8,128)(2,1)S(1)} %get-tuple-element.709), channel_id=1, source_target_pairs={{0,4},{4,8},{8,12},{12,16},{16,20},{20,24},{24,28},{28,32},{32,36}... | collective-permute-start | bytes 393224 | tf_op jit(solution)/shard_map/while/body/eval_jaxpr/ppermute | solution.py:15
  46.9 7.8 %collective-permute-start = (bf16[256,2,128]{2,0,1:T(8,128)(2,1)S(1)}, bf16[256,2,128]{2,0,1:T(8,128)(2,1)S(1)}, u32[]{:S(2)}, u32[]{:S(2)}) collective-permute-start(bf16[256,2,128]{2,0,1:T(8,128)(2,1)S(1)} %get-tuple-element.709), channel_id=1, source_target_pairs={{0,4},{4,8},{8,12},{12,16},{16,20},{20,24},{24,28},{28,32},{32,36}... | collective-permute-start | bytes 393224 | tf_op jit(solution)/shard_map/while/body/eval_jaxpr/ppermute | solution.py:15
  55.7 7.8 %collective-permute-start = (bf16[256,2,128]{2,0,1:T(8,128)(2,1)S(1)}, bf16[256,2,128]{2,0,1:T(8,128)(2,1)S(1)}, u32[]{:S(2)}, u32[]{:S(2)}) collective-permute-start(bf16[256,2,128]{2,0,1:T(8,128)(2,1)S(1)} %get-tuple-element.709), channel_id=1, source_target_pairs={{0,4},{4,8},{8,12},{12,16},{16,20},{20,24},{24,28},{28,32},{32,36}... | collective-permute-start | bytes 393224 | tf_op jit(solution)/shard_map/while/body/eval_jaxpr/ppermute | solution.py:15
  64.6 7.8 %collective-permute-start = (bf16[256,2,128]{2,0,1:T(8,128)(2,1)S(1)}, bf16[256,2,128]{2,0,1:T(8,128)(2,1)S(1)}, u32[]{:S(2)}, u32[]{:S(2)}) collective-permute-start(bf16[256,2,128]{2,0,1:T(8,128)(2,1)S(1)} %get-tuple-element.709), channel_id=1, source_target_pairs={{0,4},{4,8},{8,12},{12,16},{16,20},{20,24},{24,28},{28,32},{32,36}... | collective-permute-start | bytes 393224 | tf_op jit(solution)/shard_map/while/body/eval_jaxpr/ppermute | solution.py:15
  74.6 1.9 copy-start.15
  76.5 1.6 copy-start.2
  76.7 2.3 copy-start.17
  76.8 2.4 copy-start.21
  76.8 2.4 copy-start.24
  79.1 3.4 %copy-start.22 = (f32[2,8,256]{2,1,0:T(8,128)}, f32[2,8,256]{2,1,0:T(8,128)S(1)}, u32[]{:S(2)}) copy-start(f32[2,8,256]{2,1,0:T(8,128)S(1)} %copy.123) | copy-start | bytes 49156
  79.2 3.5 %copy-start.30 = (f32[2,256,256,8]{2,1,3,0:T(8,128)S(1)}, f32[2,256,256,8]{2,1,3,0:T(8,128)}, u32[]{:S(2)}) copy-start(f32[2,256,256,8]{2,1,3,0:T(8,128)} %get-tuple-element.597) | copy-start | bytes 12582916
  89.9 3.6 %copy-start.13 = (bf16[256,2,64]{2,0,1:T(8,128)(2,1)S(1)}, bf16[256,2,64]{2,0,1:T(8,128)(2,1)}, u32[]{:S(2)}) copy-start(bf16[256,2,64]{2,0,1:T(8,128)(2,1)} %copy-done.12) | copy-start | bytes 196612
  95.2 8.1 %collective-permute-start.1 = (bf16[256,2,2,128]{3,0,2,1:T(8,128)(2,1)}, bf16[256,2,2,128]{3,0,2,1:T(8,128)(2,1)S(1)}, u32[]{:S(2)}, u32[]{:S(2)}) collective-permute-start(bf16[256,2,2,128]{3,0,2,1:T(8,128)(2,1)} %get-tuple-element.747), channel_id=1, source_target_pairs={{0,4},{4,8},{8,12},{12,16},{16,20},{20,24},{24,28},{28,32},{32,36}... | collective-permute-start | bytes 786440 | tf_op jit(solution)/shard_map/while/body/eval_jaxpr/ppermute | solution.py:15
  95.2 14.7 %collective-permute-start.2 = (f32[256,2,2,128]{3,0,2,1:T(8,128)}, f32[256,2,2,128]{3,0,2,1:T(8,128)}, u32[]{:S(2)}, u32[]{:S(2)}) collective-permute-start(f32[256,2,2,128]{3,0,2,1:T(8,128)} %get-tuple-element.746), channel_id=1, source_target_pairs={{0,4},{4,8},{8,12},{12,16},{16,20},{20,24},{24,28},{28,32},{32,36}... | collective-permute-start | bytes 1572872 | tf_op jit(solution)/shard_map/while/body/eval_jaxpr/ppermute | solution.py:15
  103.3 1.2 copy-start.25
  111.8 9.3 %collective-permute-start.1 = (bf16[256,2,2,128]{3,0,2,1:T(8,128)(2,1)}, bf16[256,2,2,128]{3,0,2,1:T(8,128)(2,1)S(1)}, u32[]{:S(2)}, u32[]{:S(2)}) collective-permute-start(bf16[256,2,2,128]{3,0,2,1:T(8,128)(2,1)} %get-tuple-element.747), channel_id=1, source_target_pairs={{0,4},{4,8},{8,12},{12,16},{16,20},{20,24},{24,28},{28,32},{32,36}... | collective-permute-start | bytes 786440 | tf_op jit(solution)/shard_map/while/body/eval_jaxpr/ppermute | solution.py:15
  111.8 15.9 %collective-permute-start.2 = (f32[256,2,2,128]{3,0,2,1:T(8,128)}, f32[256,2,2,128]{3,0,2,1:T(8,128)}, u32[]{:S(2)}, u32[]{:S(2)}) collective-permute-start(f32[256,2,2,128]{3,0,2,1:T(8,128)} %get-tuple-element.746), channel_id=1, source_target_pairs={{0,4},{4,8},{8,12},{12,16},{16,20},{20,24},{24,28},{28,32},{32,36}... | collective-permute-start | bytes 1572872 | tf_op jit(solution)/shard_map/while/body/eval_jaxpr/ppermute | solution.py:15
  121.1 1.2 copy-start.25
  129.6 9.3 %collective-permute-start.1 = (bf16[256,2,2,128]{3,0,2,1:T(8,128)(2,1)}, bf16[256,2,2,128]{3,0,2,1:T(8,128)(2,1)S(1)}, u32[]{:S(2)}, u32[]{:S(2)}) collective-permute-start(bf16[256,2,2,128]{3,0,2,1:T(8,128)(2,1)} %get-tuple-element.747), channel_id=1, source_target_pairs={{0,4},{4,8},{8,12},{12,16},{16,20},{20,24},{24,28},{28,32},{32,36}... | collective-permute-start | bytes 786440 | tf_op jit(solution)/shard_map/while/body/eval_jaxpr/ppermute | solution.py:15
  129.6 15.9 %collective-permute-start.2 = (f32[256,2,2,128]{3,0,2,1:T(8,128)}, f32[256,2,2,128]{3,0,2,1:T(8,128)}, u32[]{:S(2)}, u32[]{:S(2)}) collective-permute-start(f32[256,2,2,128]{3,0,2,1:T(8,128)} %get-tuple-element.746), channel_id=1, source_target_pairs={{0,4},{4,8},{8,12},{12,16},{16,20},{20,24},{24,28},{28,32},{32,36}... | collective-permute-start | bytes 1572872 | tf_op jit(solution)/shard_map/while/body/eval_jaxpr/ppermute | solution.py:15
  138.9 1.2 copy-start.25
  147.4 9.3 %collective-permute-start.1 = (bf16[256,2,2,128]{3,0,2,1:T(8,128)(2,1)}, bf16[256,2,2,128]{3,0,2,1:T(8,128)(2,1)S(1)}, u32[]{:S(2)}, u32[]{:S(2)}) collective-permute-start(bf16[256,2,2,128]{3,0,2,1:T(8,128)(2,1)} %get-tuple-element.747), channel_id=1, source_target_pairs={{0,4},{4,8},{8,12},{12,16},{16,20},{20,24},{24,28},{28,32},{32,36}... | collective-permute-start | bytes 786440 | tf_op jit(solution)/shard_map/while/body/eval_jaxpr/ppermute | solution.py:15
  147.4 15.9 %collective-permute-start.2 = (f32[256,2,2,128]{3,0,2,1:T(8,128)}, f32[256,2,2,128]{3,0,2,1:T(8,128)}, u32[]{:S(2)}, u32[]{:S(2)}) collective-permute-start(f32[256,2,2,128]{3,0,2,1:T(8,128)} %get-tuple-element.746), channel_id=1, source_target_pairs={{0,4},{4,8},{8,12},{12,16},{16,20},{20,24},{24,28},{28,32},{32,36}... | collective-permute-start | bytes 1572872 | tf_op jit(solution)/shard_map/while/body/eval_jaxpr/ppermute | solution.py:15
  156.7 1.2 copy-start.25
  165.2 9.3 %collective-permute-start.1 = (bf16[256,2,2,128]{3,0,2,1:T(8,128)(2,1)}, bf16[256,2,2,128]{3,0,2,1:T(8,128)(2,1)S(1)}, u32[]{:S(2)}, u32[]{:S(2)}) collective-permute-start(bf16[256,2,2,128]{3,0,2,1:T(8,128)(2,1)} %get-tuple-element.747), channel_id=1, source_target_pairs={{0,4},{4,8},{8,12},{12,16},{16,20},{20,24},{24,28},{28,32},{32,36}... | collective-permute-start | bytes 786440 | tf_op jit(solution)/shard_map/while/body/eval_jaxpr/ppermute | solution.py:15
  165.2 15.9 %collective-permute-start.2 = (f32[256,2,2,128]{3,0,2,1:T(8,128)}, f32[256,2,2,128]{3,0,2,1:T(8,128)}, u32[]{:S(2)}, u32[]{:S(2)}) collective-permute-start(f32[256,2,2,128]{3,0,2,1:T(8,128)} %get-tuple-element.746), channel_id=1, source_target_pairs={{0,4},{4,8},{8,12},{12,16},{16,20},{20,24},{24,28},{28,32},{32,36}... | collective-permute-start | bytes 1572872 | tf_op jit(solution)/shard_map/while/body/eval_jaxpr/ppermute | solution.py:15
  183.0 9.3 %collective-permute-start.1 = (bf16[256,2,2,128]{3,0,2,1:T(8,128)(2,1)}, bf16[256,2,2,128]{3,0,2,1:T(8,128)(2,1)S(1)}, u32[]{:S(2)}, u32[]{:S(2)}) collective-permute-start(bf16[256,2,2,128]{3,0,2,1:T(8,128)(2,1)} %get-tuple-element.747), channel_id=1, source_target_pairs={{0,4},{4,8},{8,12},{12,16},{16,20},{20,24},{24,28},{28,32},{32,36}... | collective-permute-start | bytes 786440 | tf_op jit(solution)/shard_map/while/body/eval_jaxpr/ppermute | solution.py:15
  183.0 15.9 %collective-permute-start.2 = (f32[256,2,2,128]{3,0,2,1:T(8,128)}, f32[256,2,2,128]{3,0,2,1:T(8,128)}, u32[]{:S(2)}, u32[]{:S(2)}) collective-permute-start(f32[256,2,2,128]{3,0,2,1:T(8,128)} %get-tuple-element.746), channel_id=1, source_target_pairs={{0,4},{4,8},{8,12},{12,16},{16,20},{20,24},{24,28},{28,32},{32,36}... | collective-permute-start | bytes 1572872 | tf_op jit(solution)/shard_map/while/body/eval_jaxpr/ppermute | solution.py:15
  192.3 1.2 copy-start.25
  200.8 9.3 %collective-permute-start.1 = (bf16[256,2,2,128]{3,0,2,1:T(8,128)(2,1)}, bf16[256,2,2,128]{3,0,2,1:T(8,128)(2,1)S(1)}, u32[]{:S(2)}, u32[]{:S(2)}) collective-permute-start(bf16[256,2,2,128]{3,0,2,1:T(8,128)(2,1)} %get-tuple-element.747), channel_id=1, source_target_pairs={{0,4},{4,8},{8,12},{12,16},{16,20},{20,24},{24,28},{28,32},{32,36}... | collective-permute-start | bytes 786440 | tf_op jit(solution)/shard_map/while/body/eval_jaxpr/ppermute | solution.py:15
  200.8 15.9 %collective-permute-start.2 = (f32[256,2,2,128]{3,0,2,1:T(8,128)}, f32[256,2,2,128]{3,0,2,1:T(8,128)}, u32[]{:S(2)}, u32[]{:S(2)}) collective-permute-start(f32[256,2,2,128]{3,0,2,1:T(8,128)} %get-tuple-element.746), channel_id=1, source_target_pairs={{0,4},{4,8},{8,12},{12,16},{16,20},{20,24},{24,28},{28,32},{32,36}... | collective-permute-start | bytes 1572872 | tf_op jit(solution)/shard_map/while/body/eval_jaxpr/ppermute | solution.py:15
  218.6 11.3 %collective-permute-start.3 = (f32[256,2,2,128]{3,0,2,1:T(8,128)}, f32[256,2,2,128]{3,0,2,1:T(8,128)S(1)}, u32[]{:S(2)}, u32[]{:S(2)}) collective-permute-start(f32[256,2,2,128]{3,0,2,1:T(8,128)} %get-tuple-element.450), channel_id=1, source_target_pairs={{0,228},{4,232},{8,236},{12,240},{16,244},{20,248},{24,252},{28,0}... | collective-permute-start | bytes 1572872 | tf_op jit(solution)/shard_map/ppermute | solution.py:15
  220.2 2.5 copy-start.1
  220.2 2.5 copy-start.9
  220.2 2.5 copy-start.27
  224.8 1.2 copy-start.3
  226.0 3.8 %copy-start.29 = (f32[128]{0:T(128)S(1)}, f32[128]{0:T(128)}, u32[]{:S(2)}) copy-start(f32[128]{0:T(128)} %param.18) | copy-start | bytes 1540
  226.0 4.0 %copy-start.7 = (f32[256,2,128]{2,0,1:T(8,128)S(1)}, f32[256,2,128]{2,0,1:T(8,128)}, u32[]{:S(2)}) copy-start(f32[256,2,128]{2,0,1:T(8,128)} %copy-done.6) | copy-start | bytes 786436
  (23 other events, 25.7 us)
where the time goes:
time: 318 us; the launch traced here: 317 us
  waiting for transfers between devices  94.1 us (30%)
  blocking collectives  84 us (26%)
  matrix products  54.6 us (17%)
  other arithmetic  39.4 us (12%)
  local copies, waits for them, and re-layouts  36.9 us (12%)
  starting transfers between devices  5.57 us (2%)
    ppermute x22, waiting for transfers between devices, passed_along(): return lax.ppermute(value, axis, pairs)  94.1 us
    psum x1, blocking collectives, on_device(): lax.psum((q_gain_part, k_gain_part), ('ctx', 'heads'))  84 us
    dot_general x15, matrix products, scores_of(): jnp.einsum('ikgd,jkd->kgij', q_rot, key_rot, preferred_element_type=jnp.f...  15 us
    unnamed x68, local copies, waits for them, and re-layouts  13.6 us
    add x7, other arithmetic, back_step(): grads_now = passed_along(grads_now, 'ctx', 1) + kv_part  13.4 us
    dot_general x8, matrix products, grad_terms(): jnp.einsum('ikgd,jkd->kgij', grad_heads, val_rot, preferred_element_type=...  12.1 us
    dot_general x8, matrix products, grad_terms(): jnp.einsum('kgij,jkd->ikgd', dscore, key_rot, preferred_element_type=jnp....  11.6 us
    dot_general x8, matrix products, grad_terms(): jnp.einsum('kgij,ikgd->jkd', weights_low, grad_heads, preferred_element_t...  10 us
  transfers between devices with their start and end apart: 22, of which 14 were waited for; matrix products, arithmetic and copies ran while one was open for 22% of the time, Pallas kernels for 0%

commit v1 on v0

--- a/solution.py
+++ b/solution.py
@@ -163,7 +163,7 @@
     dq_rot = dq_acc.reshape(tokens_here, kv_local * group_size, head_dim)
     dq_input, q_gain_part = norm_rope_back(q_float, q_gain, cos_table, sin_table, dq_rot)
     dk_input, k_gain_part = norm_rope_back(k_float, k_gain, cos_table, sin_table, key_grads[:, 0])
-    q_gain_grad, k_gain_grad = lax.psum((q_gain_part, k_gain_part), ("ctx", "heads"))
+    q_gain_grad, k_gain_grad = lax.psum(lax.psum((q_gain_part, k_gain_part), "ctx"), "heads")
     dq_raw = dq_input.astype(jnp.bfloat16).reshape(tokens_here, kv_local * group_size * head_dim)
     dk_raw = dk_input.astype(jnp.bfloat16).reshape(tokens_here, kv_local * head_dim)
     dv = key_grads[:, 1].astype(jnp.bfloat16).reshape(tokens_here, kv_local * head_dim)

time: 318 us -> 378 us (1.19)
  blocking collectives: 84 us -> 141 us
    psum x1 -> x2, blocking collectives: 84 us -> 141 us  [the longest x1 131 us: on_device(): lax.psum((q_gain_part, k_gain_part), 'ctx')]
    unnamed x68 -> x72, local copies, waits for them, and re-layouts: 13.6 us -> 14.1 us
  transfers between devices with their start and end apart: 22 -> 22, of which waited for: 14 -> 14; matrix products, arithmetic and copies ran while one was open for 22% -> 18% of each run, Pallas kernels for 0% -> 0%
where the time goes in v1:
time: 378 us; the launch traced here: 377 us
  blocking collectives  141 us (37%)
  waiting for transfers between devices  94 us (25%)
  matrix products  54.6 us (14%)
  other arithmetic  40.2 us (11%)
  local copies, waits for them, and re-layouts  39.3 us (10%)
  starting transfers between devices  5.64 us (1%)
    psum x1, blocking collectives, on_device(): lax.psum((q_gain_part, k_gain_part), 'ctx')  131 us
    ppermute x22, waiting for transfers between devices, passed_along(): return lax.ppermute(value, axis, pairs)  94 us
    dot_general x15, matrix products, scores_of(): jnp.einsum('ikgd,jkd->kgij', q_rot, key_rot, preferred_element_type=jnp.f...  15 us
    unnamed x72, local copies, waits for them, and re-layouts  14.1 us
    add x7, other arithmetic, back_step(): grads_now = passed_along(grads_now, 'ctx', 1) + kv_part  13.4 us
    dot_general x8, matrix products, grad_terms(): jnp.einsum('ikgd,jkd->kgij', grad_heads, val_rot, preferred_element_type=...  12.1 us
    dot_general x8, matrix products, grad_terms(): jnp.einsum('kgij,jkd->ikgd', dscore, key_rot, preferred_element_type=jnp....  11.6 us
    dot_general x8, matrix products, grad_terms(): jnp.einsum('kgij,ikgd->jkd', weights_low, grad_heads, preferred_element_t...  10 us
  transfers between devices with their start and end apart: 22, of which 14 were waited for; matrix products, arithmetic and copies ran while one was open for 18% of the time, Pallas kernels for 0%

profile of v1, /device:TPU:1, one launch (start us, length us, event | category | flops | bytes accessed | tf_op | source)
XLA Modules:
  0.0 376.6 jit_solution(6099821067665270080)
XLA Ops:
  2.8 1.5 convert_bitcast_fusion
  11.5 2.9 fusion.29
  14.4 59.1 %while.38 = (s32[]{:T(128)}, f32[2,8,256]{2,1,0:T(8,128)S(1)}, bf16[256,2,128]{2,0,1:T(8,128)(2,1)S(1)}, s32[4,32]{1,0:T(4,128)S(1)}, s32[]{:T(128)}, /*index=5*...) while((s32[]{:T(128)}, f32[2,8,256]{2,1,0:T(8,128)S(1)}, ...), condition=%wide.region_8.9_spmd.clone, body=%wide.region_5.8_spmd.clone.sunk | while | flops 271778816 | bytes 2167688 | solution.py:125
  14.4 2.7 collective-permute-start
  20.1 2.5 collective-permute-start
  23.2 4.9 %collective-permute-done = bf16[256,2,128]{2,0,1:T(8,128)(2,1)S(1)} collective-permute-done((bf16[256,2,128]{2,0,1:T(8,128)(2,1)S(1)}, bf16[256,2,128]{2,0,1:T(8,128)(2,1)S(1)}, u32[]{:S(2)}, u32[]{:S(2)}) %collective-permute-start) | collective-permute-done | bytes 131104 | tf_op jit(solution)/shard_map/while/body/eval_jaxpr/ppermute | solution.py:15
  29.9 7.1 %collective-permute-done = bf16[256,2,128]{2,0,1:T(8,128)(2,1)S(1)} collective-permute-done((bf16[256,2,128]{2,0,1:T(8,128)(2,1)S(1)}, bf16[256,2,128]{2,0,1:T(8,128)(2,1)S(1)}, u32[]{:S(2)}, u32[]{:S(2)}) %collective-permute-start) | collective-permute-done | bytes 131104 | tf_op jit(solution)/shard_map/while/body/eval_jaxpr/ppermute | solution.py:15
  38.8 7.1 %collective-permute-done = bf16[256,2,128]{2,0,1:T(8,128)(2,1)S(1)} collective-permute-done((bf16[256,2,128]{2,0,1:T(8,128)(2,1)S(1)}, bf16[256,2,128]{2,0,1:T(8,128)(2,1)S(1)}, u32[]{:S(2)}, u32[]{:S(2)}) %collective-permute-start) | collective-permute-done | bytes 131104 | tf_op jit(solution)/shard_map/while/body/eval_jaxpr/ppermute | solution.py:15
  47.6 7.1 %collective-permute-done = bf16[256,2,128]{2,0,1:T(8,128)(2,1)S(1)} collective-permute-done((bf16[256,2,128]{2,0,1:T(8,128)(2,1)S(1)}, bf16[256,2,128]{2,0,1:T(8,128)(2,1)S(1)}, u32[]{:S(2)}, u32[]{:S(2)}) %collective-permute-start) | collective-permute-done | bytes 131104 | tf_op jit(solution)/shard_map/while/body/eval_jaxpr/ppermute | solution.py:15
  56.5 7.1 %collective-permute-done = bf16[256,2,128]{2,0,1:T(8,128)(2,1)S(1)} collective-permute-done((bf16[256,2,128]{2,0,1:T(8,128)(2,1)S(1)}, bf16[256,2,128]{2,0,1:T(8,128)(2,1)S(1)}, u32[]{:S(2)}, u32[]{:S(2)}) %collective-permute-start) | collective-permute-done | bytes 131104 | tf_op jit(solution)/shard_map/while/body/eval_jaxpr/ppermute | solution.py:15
  65.4 7.1 %collective-permute-done = bf16[256,2,128]{2,0,1:T(8,128)(2,1)S(1)} collective-permute-done((bf16[256,2,128]{2,0,1:T(8,128)(2,1)S(1)}, bf16[256,2,128]{2,0,1:T(8,128)(2,1)S(1)}, u32[]{:S(2)}, u32[]{:S(2)}) %collective-permute-start) | collective-permute-done | bytes 131104 | tf_op jit(solution)/shard_map/while/body/eval_jaxpr/ppermute | solution.py:15
  74.7 1.9 copy.122
  76.6 1.6 copy.142
  78.5 1.6 multiply_reduce_fusion
  81.3 3.3 fusion.40
  84.8 1.5 fusion.27
  87.2 1.8 convolution_bitcast_fusion.1
  92.1 1.9 copy.98
  94.1 1.7 copy.97
  95.7 1.7 pad_maximum_fusion.3
  97.4 123.4 %while.39 = (s32[]{:T(128)}, f32[256,2,8,128]{3,0,2,1:T(8,128)S(1)}, f32[256,2,2,128]{3,0,2,1:T(8,128)}, bf16[256,2,2,128]{3,0,2,1:T(8,128)(2,1)}, s32[4,32]{1,0...) while((s32[]{:T(128)}, ...), condition=%wide.region_11.12_spmd.clone, body=%wide.region_9.11_spmd.clone.sunk | while | flops 1354695680 | bytes 37999652 | solution.py:159
  99.1 6.4 %collective-permute-done.1 = bf16[256,2,2,128]{3,0,2,1:T(8,128)(2,1)S(1)} collective-permute-done((bf16[256,2,2,128]{3,0,2,1:T(8,128)(2,1)}, bf16[256,2,2,128]{3,0,2,1:T(8,128)(2,1)S(1)}, u32[]{:S(2)}, u32[]{:S(2)}) %collective-permute-start.1) | collective-permute-done | bytes 262176 | tf_op jit(solution)/shard_map/while/body/eval_jaxpr/ppermute | solution.py:15
  106.8 1.5 fusion.95
  112.1 1.9 maximum_add_fusion.2
  115.7 7.6 %collective-permute-done.1 = bf16[256,2,2,128]{3,0,2,1:T(8,128)(2,1)S(1)} collective-permute-done((bf16[256,2,2,128]{3,0,2,1:T(8,128)(2,1)}, bf16[256,2,2,128]{3,0,2,1:T(8,128)(2,1)S(1)}, u32[]{:S(2)}, u32[]{:S(2)}) %collective-permute-start.1) | collective-permute-done | bytes 262176 | tf_op jit(solution)/shard_map/while/body/eval_jaxpr/ppermute | solution.py:15
  124.6 1.5 fusion.95
  129.9 1.9 maximum_add_fusion.2
  133.5 7.6 %collective-permute-done.1 = bf16[256,2,2,128]{3,0,2,1:T(8,128)(2,1)S(1)} collective-permute-done((bf16[256,2,2,128]{3,0,2,1:T(8,128)(2,1)}, bf16[256,2,2,128]{3,0,2,1:T(8,128)(2,1)S(1)}, u32[]{:S(2)}, u32[]{:S(2)}) %collective-permute-start.1) | collective-permute-done | bytes 262176 | tf_op jit(solution)/shard_map/while/body/eval_jaxpr/ppermute | solution.py:15
  142.3 1.5 fusion.95
  147.7 1.9 maximum_add_fusion.2
  151.3 7.6 %collective-permute-done.1 = bf16[256,2,2,128]{3,0,2,1:T(8,128)(2,1)S(1)} collective-permute-done((bf16[256,2,2,128]{3,0,2,1:T(8,128)(2,1)}, bf16[256,2,2,128]{3,0,2,1:T(8,128)(2,1)S(1)}, u32[]{:S(2)}, u32[]{:S(2)}) %collective-permute-start.1) | collective-permute-done | bytes 262176 | tf_op jit(solution)/shard_map/while/body/eval_jaxpr/ppermute | solution.py:15
  160.1 1.5 fusion.95
  165.5 1.9 maximum_add_fusion.2
  169.1 7.6 %collective-permute-done.1 = bf16[256,2,2,128]{3,0,2,1:T(8,128)(2,1)S(1)} collective-permute-done((bf16[256,2,2,128]{3,0,2,1:T(8,128)(2,1)}, bf16[256,2,2,128]{3,0,2,1:T(8,128)(2,1)S(1)}, u32[]{:S(2)}, u32[]{:S(2)}) %collective-permute-start.1) | collective-permute-done | bytes 262176 | tf_op jit(solution)/shard_map/while/body/eval_jaxpr/ppermute | solution.py:15
  177.9 1.5 fusion.95
  179.5 1.4 bitcast_add_fusion.2
  183.3 1.9 maximum_add_fusion.2
  186.9 7.6 %collective-permute-done.1 = bf16[256,2,2,128]{3,0,2,1:T(8,128)(2,1)S(1)} collective-permute-done((bf16[256,2,2,128]{3,0,2,1:T(8,128)(2,1)}, bf16[256,2,2,128]{3,0,2,1:T(8,128)(2,1)S(1)}, u32[]{:S(2)}, u32[]{:S(2)}) %collective-permute-start.1) | collective-permute-done | bytes 262176 | tf_op jit(solution)/shard_map/while/body/eval_jaxpr/ppermute | solution.py:15
  195.7 1.5 fusion.95
  201.1 1.9 maximum_add_fusion.2
  204.7 7.6 %collective-permute-done.1 = bf16[256,2,2,128]{3,0,2,1:T(8,128)(2,1)S(1)} collective-permute-done((bf16[256,2,2,128]{3,0,2,1:T(8,128)(2,1)}, bf16[256,2,2,128]{3,0,2,1:T(8,128)(2,1)S(1)}, u32[]{:S(2)}, u32[]{:S(2)}) %collective-permute-start.1) | collective-permute-done | bytes 262176 | tf_op jit(solution)/shard_map/while/body/eval_jaxpr/ppermute | solution.py:15
  213.5 1.5 fusion.95
  218.9 1.9 maximum_add_fusion.2
  222.3 2.5 multiply_add_fusion
  224.9 2.1 multiply_reduce_fusion.1
  228.3 3.8 %fusion.36 = (f32[2048]{0:T(1024)S(1)}, bf16[256,2048]{1,0:T(8,128)(2,1)}) fusion(bf16[256,2048]{1,0:T(8,128)(2,1)S(1)} %copy-done.3, f32[32,8,16,128]{3,2,1,0:T(8,128)S(1)} %bitcast.265, f32[32,8,16,128]{3,2,1,0:T(8,128)S(1)} %bitcast.267, f32[32,8,16,128]{3,2,1,0:T(8,128)S(1)} %bitcast.266, f32[2048]{0:T(1024)S(1)} %broadcast_bitcast_fusion), kind=kLoop, calls=%fused_computation.53 | loop fusion | flops 4716544 | bytes 8404992 | tf_op jit(solution)/shard_map/reduce_sum | solution.py:59
  235.9 131.5 %all-reduce = (f32[128]{0:T(128)S(1)}, f32[128]{0:T(128)S(1)}) all-reduce(f32[128]{0:T(128)S(1)} %bitcast_reduce_fusion, f32[128]{0:T(128)S(1)} %bitcast_reduce_fusion.1), channel_id=1, replica_groups=mesh['ctx'=64,'heads'=4] {'ctx'}, use_global_device_ids=true, to_apply=%region_16.17 | all-reduce | flops 256 | bytes 2048 | tf_op jit(solution)/shard_map/psum | solution.py:166
  367.4 9.2 %all-reduce.1 = (f32[128]{0:T(128)}, f32[128]{0:T(128)}) all-reduce(f32[128]{0:T(128)S(1)} %get-tuple-element.574, f32[128]{0:T(128)S(1)} %get-tuple-element.575), channel_id=1, replica_groups=mesh['ctx'=64,'heads'=4] {'heads'}, use_global_device_ids=true, to_apply=%region_17.18 | all-reduce | flops 256 | bytes 2048 | tf_op jit(solution)/shard_map/psum | solution.py:166
  (325 shorter events, 80.8 us)
Async XLA Ops:
  1.8 5.1 %copy-start.6 = (f32[256,2,128]{2,0,1:T(8,128)}, f32[256,2,128]{2,0,1:T(8,128)S(1)}, u32[]{:S(2)}) copy-start(f32[256,2,128]{2,0,1:T(8,128)S(1)} %copy.83) | copy-start | bytes 786436
  4.7 2.2 copy-start
  4.7 1.3 copy-start.28
  7.2 2.6 copy-start.14
  10.0 4.4 %copy-start.12 = (bf16[256,2,128]{2,0,1:T(8,128)(2,1)}, bf16[256,2,128]{2,0,1:T(8,128)(2,1)S(1)}, u32[]{:S(2)}) copy-start(bf16[256,2,128]{2,0,1:T(8,128)(2,1)S(1)} %pad_maximum_fusion.5) | copy-start | bytes 393220
  11.5 2.9 copy-start.21
  14.4 59.8 %copy-start.16 = (bf16[256,2048]{1,0:T(8,128)(2,1)S(1)}, bf16[256,2048]{1,0:T(8,128)(2,1)}, u32[]{:S(2)}) copy-start(bf16[256,2048]{1,0:T(8,128)(2,1)} %param.16) | copy-start | bytes 3145732
  14.4 4.6 %collective-permute-start = (bf16[256,2,128]{2,0,1:T(8,128)(2,1)S(1)}, bf16[256,2,128]{2,0,1:T(8,128)(2,1)S(1)}, u32[]{:S(2)}, u32[]{:S(2)}) collective-permute-start(bf16[256,2,128]{2,0,1:T(8,128)(2,1)S(1)} %get-tuple-element.711), channel_id=1, source_target_pairs={{0,4},{4,8},{8,12},{12,16},{16,20},{20,24},{24,28},{28,32},{32,36}... | collective-permute-start | bytes 393224 | tf_op jit(solution)/shard_map/while/body/eval_jaxpr/ppermute | solution.py:15
  20.1 8.0 %collective-permute-start = (bf16[256,2,128]{2,0,1:T(8,128)(2,1)S(1)}, bf16[256,2,128]{2,0,1:T(8,128)(2,1)S(1)}, u32[]{:S(2)}, u32[]{:S(2)}) collective-permute-start(bf16[256,2,128]{2,0,1:T(8,128)(2,1)S(1)} %get-tuple-element.711), channel_id=1, source_target_pairs={{0,4},{4,8},{8,12},{12,16},{16,20},{20,24},{24,28},{28,32},{32,36}... | collective-permute-start | bytes 393224 | tf_op jit(solution)/shard_map/while/body/eval_jaxpr/ppermute | solution.py:15
  29.2 7.8 %collective-permute-start = (bf16[256,2,128]{2,0,1:T(8,128)(2,1)S(1)}, bf16[256,2,128]{2,0,1:T(8,128)(2,1)S(1)}, u32[]{:S(2)}, u32[]{:S(2)}) collective-permute-start(bf16[256,2,128]{2,0,1:T(8,128)(2,1)S(1)} %get-tuple-element.711), channel_id=1, source_target_pairs={{0,4},{4,8},{8,12},{12,16},{16,20},{20,24},{24,28},{28,32},{32,36}... | collective-permute-start | bytes 393224 | tf_op jit(solution)/shard_map/while/body/eval_jaxpr/ppermute | solution.py:15
  38.1 7.8 %collective-permute-start = (bf16[256,2,128]{2,0,1:T(8,128)(2,1)S(1)}, bf16[256,2,128]{2,0,1:T(8,128)(2,1)S(1)}, u32[]{:S(2)}, u32[]{:S(2)}) collective-permute-start(bf16[256,2,128]{2,0,1:T(8,128)(2,1)S(1)} %get-tuple-element.711), channel_id=1, source_target_pairs={{0,4},{4,8},{8,12},{12,16},{16,20},{20,24},{24,28},{28,32},{32,36}... | collective-permute-start | bytes 393224 | tf_op jit(solution)/shard_map/while/body/eval_jaxpr/ppermute | solution.py:15
  47.0 7.8 %collective-permute-start = (bf16[256,2,128]{2,0,1:T(8,128)(2,1)S(1)}, bf16[256,2,128]{2,0,1:T(8,128)(2,1)S(1)}, u32[]{:S(2)}, u32[]{:S(2)}) collective-permute-start(bf16[256,2,128]{2,0,1:T(8,128)(2,1)S(1)} %get-tuple-element.711), channel_id=1, source_target_pairs={{0,4},{4,8},{8,12},{12,16},{16,20},{20,24},{24,28},{28,32},{32,36}... | collective-permute-start | bytes 393224 | tf_op jit(solution)/shard_map/while/body/eval_jaxpr/ppermute | solution.py:15
  55.8 7.8 %collective-permute-start = (bf16[256,2,128]{2,0,1:T(8,128)(2,1)S(1)}, bf16[256,2,128]{2,0,1:T(8,128)(2,1)S(1)}, u32[]{:S(2)}, u32[]{:S(2)}) collective-permute-start(bf16[256,2,128]{2,0,1:T(8,128)(2,1)S(1)} %get-tuple-element.711), channel_id=1, source_target_pairs={{0,4},{4,8},{8,12},{12,16},{16,20},{20,24},{24,28},{28,32},{32,36}... | collective-permute-start | bytes 393224 | tf_op jit(solution)/shard_map/while/body/eval_jaxpr/ppermute | solution.py:15
  64.7 7.8 %collective-permute-start = (bf16[256,2,128]{2,0,1:T(8,128)(2,1)S(1)}, bf16[256,2,128]{2,0,1:T(8,128)(2,1)S(1)}, u32[]{:S(2)}, u32[]{:S(2)}) collective-permute-start(bf16[256,2,128]{2,0,1:T(8,128)(2,1)S(1)} %get-tuple-element.711), channel_id=1, source_target_pairs={{0,4},{4,8},{8,12},{12,16},{16,20},{20,24},{24,28},{28,32},{32,36}... | collective-permute-start | bytes 393224 | tf_op jit(solution)/shard_map/while/body/eval_jaxpr/ppermute | solution.py:15
  76.6 1.9 copy-start.2
  78.2 3.0 copy-start.18
  81.2 3.4 copy-start.24
  81.2 3.4 copy-start.23
  81.2 3.4 copy-start.26
  81.2 3.5 copy-start.32
  92.1 3.6 copy-start.15
  97.4 8.1 %collective-permute-start.1 = (bf16[256,2,2,128]{3,0,2,1:T(8,128)(2,1)}, bf16[256,2,2,128]{3,0,2,1:T(8,128)(2,1)S(1)}, u32[]{:S(2)}, u32[]{:S(2)}) collective-permute-start(bf16[256,2,2,128]{3,0,2,1:T(8,128)(2,1)} %get-tuple-element.749), channel_id=1, source_target_pairs={{0,4},{4,8},{8,12},{12,16},{16,20},{20,24},{24,28},{28,32},{32,36}... | collective-permute-start | bytes 786440 | tf_op jit(solution)/shard_map/while/body/eval_jaxpr/ppermute | solution.py:15
  97.4 14.7 %collective-permute-start.2 = (f32[256,2,2,128]{3,0,2,1:T(8,128)}, f32[256,2,2,128]{3,0,2,1:T(8,128)}, u32[]{:S(2)}, u32[]{:S(2)}) collective-permute-start(f32[256,2,2,128]{3,0,2,1:T(8,128)} %get-tuple-element.748), channel_id=1, source_target_pairs={{0,4},{4,8},{8,12},{12,16},{16,20},{20,24},{24,28},{28,32},{32,36}... | collective-permute-start | bytes 1572872 | tf_op jit(solution)/shard_map/while/body/eval_jaxpr/ppermute | solution.py:15
  105.5 1.2 copy-start.27
  114.0 9.3 %collective-permute-start.1 = (bf16[256,2,2,128]{3,0,2,1:T(8,128)(2,1)}, bf16[256,2,2,128]{3,0,2,1:T(8,128)(2,1)S(1)}, u32[]{:S(2)}, u32[]{:S(2)}) collective-permute-start(bf16[256,2,2,128]{3,0,2,1:T(8,128)(2,1)} %get-tuple-element.749), channel_id=1, source_target_pairs={{0,4},{4,8},{8,12},{12,16},{16,20},{20,24},{24,28},{28,32},{32,36}... | collective-permute-start | bytes 786440 | tf_op jit(solution)/shard_map/while/body/eval_jaxpr/ppermute | solution.py:15
  114.0 15.9 %collective-permute-start.2 = (f32[256,2,2,128]{3,0,2,1:T(8,128)}, f32[256,2,2,128]{3,0,2,1:T(8,128)}, u32[]{:S(2)}, u32[]{:S(2)}) collective-permute-start(f32[256,2,2,128]{3,0,2,1:T(8,128)} %get-tuple-element.748), channel_id=1, source_target_pairs={{0,4},{4,8},{8,12},{12,16},{16,20},{20,24},{24,28},{28,32},{32,36}... | collective-permute-start | bytes 1572872 | tf_op jit(solution)/shard_map/while/body/eval_jaxpr/ppermute | solution.py:15
  123.3 1.2 copy-start.27
  131.8 9.3 %collective-permute-start.1 = (bf16[256,2,2,128]{3,0,2,1:T(8,128)(2,1)}, bf16[256,2,2,128]{3,0,2,1:T(8,128)(2,1)S(1)}, u32[]{:S(2)}, u32[]{:S(2)}) collective-permute-start(bf16[256,2,2,128]{3,0,2,1:T(8,128)(2,1)} %get-tuple-element.749), channel_id=1, source_target_pairs={{0,4},{4,8},{8,12},{12,16},{16,20},{20,24},{24,28},{28,32},{32,36}... | collective-permute-start | bytes 786440 | tf_op jit(solution)/shard_map/while/body/eval_jaxpr/ppermute | solution.py:15
  131.8 15.9 %collective-permute-start.2 = (f32[256,2,2,128]{3,0,2,1:T(8,128)}, f32[256,2,2,128]{3,0,2,1:T(8,128)}, u32[]{:S(2)}, u32[]{:S(2)}) collective-permute-start(f32[256,2,2,128]{3,0,2,1:T(8,128)} %get-tuple-element.748), channel_id=1, source_target_pairs={{0,4},{4,8},{8,12},{12,16},{16,20},{20,24},{24,28},{28,32},{32,36}... | collective-permute-start | bytes 1572872 | tf_op jit(solution)/shard_map/while/body/eval_jaxpr/ppermute | solution.py:15
  141.1 1.2 copy-start.27
  149.6 9.3 %collective-permute-start.1 = (bf16[256,2,2,128]{3,0,2,1:T(8,128)(2,1)}, bf16[256,2,2,128]{3,0,2,1:T(8,128)(2,1)S(1)}, u32[]{:S(2)}, u32[]{:S(2)}) collective-permute-start(bf16[256,2,2,128]{3,0,2,1:T(8,128)(2,1)} %get-tuple-element.749), channel_id=1, source_target_pairs={{0,4},{4,8},{8,12},{12,16},{16,20},{20,24},{24,28},{28,32},{32,36}... | collective-permute-start | bytes 786440 | tf_op jit(solution)/shard_map/while/body/eval_jaxpr/ppermute | solution.py:15
  149.6 15.9 %collective-permute-start.2 = (f32[256,2,2,128]{3,0,2,1:T(8,128)}, f32[256,2,2,128]{3,0,2,1:T(8,128)}, u32[]{:S(2)}, u32[]{:S(2)}) collective-permute-start(f32[256,2,2,128]{3,0,2,1:T(8,128)} %get-tuple-element.748), channel_id=1, source_target_pairs={{0,4},{4,8},{8,12},{12,16},{16,20},{20,24},{24,28},{28,32},{32,36}... | collective-permute-start | bytes 1572872 | tf_op jit(solution)/shard_map/while/body/eval_jaxpr/ppermute | solution.py:15
  158.9 1.2 copy-start.27
  167.4 9.3 %collective-permute-start.1 = (bf16[256,2,2,128]{3,0,2,1:T(8,128)(2,1)}, bf16[256,2,2,128]{3,0,2,1:T(8,128)(2,1)S(1)}, u32[]{:S(2)}, u32[]{:S(2)}) collective-permute-start(bf16[256,2,2,128]{3,0,2,1:T(8,128)(2,1)} %get-tuple-element.749), channel_id=1, source_target_pairs={{0,4},{4,8},{8,12},{12,16},{16,20},{20,24},{24,28},{28,32},{32,36}... | collective-permute-start | bytes 786440 | tf_op jit(solution)/shard_map/while/body/eval_jaxpr/ppermute | solution.py:15
  167.4 15.9 %collective-permute-start.2 = (f32[256,2,2,128]{3,0,2,1:T(8,128)}, f32[256,2,2,128]{3,0,2,1:T(8,128)}, u32[]{:S(2)}, u32[]{:S(2)}) collective-permute-start(f32[256,2,2,128]{3,0,2,1:T(8,128)} %get-tuple-element.748), channel_id=1, source_target_pairs={{0,4},{4,8},{8,12},{12,16},{16,20},{20,24},{24,28},{28,32},{32,36}... | collective-permute-start | bytes 1572872 | tf_op jit(solution)/shard_map/while/body/eval_jaxpr/ppermute | solution.py:15
  176.7 1.2 copy-start.27
  185.2 9.3 %collective-permute-start.1 = (bf16[256,2,2,128]{3,0,2,1:T(8,128)(2,1)}, bf16[256,2,2,128]{3,0,2,1:T(8,128)(2,1)S(1)}, u32[]{:S(2)}, u32[]{:S(2)}) collective-permute-start(bf16[256,2,2,128]{3,0,2,1:T(8,128)(2,1)} %get-tuple-element.749), channel_id=1, source_target_pairs={{0,4},{4,8},{8,12},{12,16},{16,20},{20,24},{24,28},{28,32},{32,36}... | collective-permute-start | bytes 786440 | tf_op jit(solution)/shard_map/while/body/eval_jaxpr/ppermute | solution.py:15
  185.2 15.9 %collective-permute-start.2 = (f32[256,2,2,128]{3,0,2,1:T(8,128)}, f32[256,2,2,128]{3,0,2,1:T(8,128)}, u32[]{:S(2)}, u32[]{:S(2)}) collective-permute-start(f32[256,2,2,128]{3,0,2,1:T(8,128)} %get-tuple-element.748), channel_id=1, source_target_pairs={{0,4},{4,8},{8,12},{12,16},{16,20},{20,24},{24,28},{28,32},{32,36}... | collective-permute-start | bytes 1572872 | tf_op jit(solution)/shard_map/while/body/eval_jaxpr/ppermute | solution.py:15
  194.5 1.2 copy-start.27
  203.0 9.3 %collective-permute-start.1 = (bf16[256,2,2,128]{3,0,2,1:T(8,128)(2,1)}, bf16[256,2,2,128]{3,0,2,1:T(8,128)(2,1)S(1)}, u32[]{:S(2)}, u32[]{:S(2)}) collective-permute-start(bf16[256,2,2,128]{3,0,2,1:T(8,128)(2,1)} %get-tuple-element.749), channel_id=1, source_target_pairs={{0,4},{4,8},{8,12},{12,16},{16,20},{20,24},{24,28},{28,32},{32,36}... | collective-permute-start | bytes 786440 | tf_op jit(solution)/shard_map/while/body/eval_jaxpr/ppermute | solution.py:15
  203.0 15.9 %collective-permute-start.2 = (f32[256,2,2,128]{3,0,2,1:T(8,128)}, f32[256,2,2,128]{3,0,2,1:T(8,128)}, u32[]{:S(2)}, u32[]{:S(2)}) collective-permute-start(f32[256,2,2,128]{3,0,2,1:T(8,128)} %get-tuple-element.748), channel_id=1, source_target_pairs={{0,4},{4,8},{8,12},{12,16},{16,20},{20,24},{24,28},{28,32},{32,36}... | collective-permute-start | bytes 1572872 | tf_op jit(solution)/shard_map/while/body/eval_jaxpr/ppermute | solution.py:15
  220.8 11.4 %collective-permute-start.3 = (f32[256,2,2,128]{3,0,2,1:T(8,128)}, f32[256,2,2,128]{3,0,2,1:T(8,128)S(1)}, u32[]{:S(2)}, u32[]{:S(2)}) collective-permute-start(f32[256,2,2,128]{3,0,2,1:T(8,128)} %get-tuple-element.450), channel_id=1, source_target_pairs={{0,228},{4,232},{8,236},{12,240},{16,244},{20,248},{24,252},{28,0}... | collective-permute-start | bytes 1572872 | tf_op jit(solution)/shard_map/ppermute | solution.py:15
  222.3 2.5 copy-start.1
  222.3 2.5 copy-start.9
  222.3 2.5 copy-start.29
  227.0 1.2 copy-start.3
  228.3 3.8 %copy-start.31 = (f32[128]{0:T(128)S(1)}, f32[128]{0:T(128)}, u32[]{:S(2)}) copy-start(f32[128]{0:T(128)} %param.18) | copy-start | bytes 1540
  228.3 4.1 %copy-start.7 = (f32[256,2,128]{2,0,1:T(8,128)S(1)}, f32[256,2,128]{2,0,1:T(8,128)}, u32[]{:S(2)}) copy-start(f32[256,2,128]{2,0,1:T(8,128)} %copy-done.6) | copy-start | bytes 786436
  (25 other events, 27.4 us)
